TPU v7x, 32 devices: a whole 2x2x4 slice. The times are simulated.
32 devices in a mesh: block: 8 (over z, x), tm: 4 (over y, core).
Axes of the slice: x: 2, y: 2, z: 4, core: 2. Of those that a mesh axis runs over, the one named last changes fastest.
Arguments:
- traces: float32 [256, 8192], P('block', 'tm'), may hold values from -600 to 600, as said below
- partners: int32 [2, 8], replicated, may hold values from 0 to 7, as said below
- slab_lengths: int32 [4], replicated, may hold values from 1024 to 2048, as said below
Outputs:
- correlations: float32 [256, 101, 3, 32], P(('block', 'tm'))
Inputs may be any that keep to these rules, and one draw needn't show every extreme that they name: partners[r, b] = b XOR m_r, where m_r is a nonzero number below 8, the same for every block and different in every round; one of the rounds has m_r = 4. `slab_lengths`: some slab is complete and some slab holds exactly 1024 recorded samples. `traces`: real values.
All inputs are finite; a program needn't handle non-finite values.
Results may differ from a plain program's by a relative error of at most 0.0041.
Values may be sent and summed in bfloat16 or wider, within the bound.
A program may use at most 64 MiB of HBM per device.

v0:
```python
import functools

import jax
import jax.numpy as jnp
from jax import lax
from jax.experimental import pallas as pl
from jax.experimental.pallas import tpu as pltpu
from jax.sharding import PartitionSpec as P

HALF = 50
ROUNDS = 2
LAGS = 101
FINE = 8
COARSE = 13
PAD = 128
CHUNKS = 8
MESH = pl.DeviceIdType.MESH


def kernel(
    nb, nt, rows, width,
    traces_ref, partners_ref, lengths_ref, out_ref,
    raw, edge, esend, erecv, ext, lhs, rhs, padded, cross, hops, norms, part, parts,
    load_sem, esend_sem, erecv_sem, hsend_sem, hrecv_sem,
    csend_sem, crecv_sem, bsend_sem, brecv_sem,
    nsend_sem, nrecv_sem, psend_sem, precv_sem,
):
    b = lax.axis_index("block")
    t = lax.axis_index("tm")
    bits = nb.bit_length() - 2
    half_mask = nb // 2
    share = rows // nt
    chunk = width // CHUNKS
    span = width + PAD
    f32, bf16 = jnp.float32, jnp.bfloat16

    def at_tm(i):
        return (b, lax.rem(t + i, nt))

    def flip(mask):
        size = 2 * mask
        low = lax.rem(b, size)
        return (b - low + lax.rem(low + mask, size), t)

    barrier = pltpu.get_barrier_semaphore()
    load = pltpu.make_async_copy(traces_ref, raw, load_sem)
    load.start()
    peers = [at_tm(i) for i in range(1, nt)] + [flip(1 << i) for i in range(bits + 1)]
    for peer in peers:
        pl.semaphore_signal(barrier, inc=1, device_id=peer, device_id_type=MESH)

    def gap(values, index, first):
        length = lengths_ref[index]
        begin = length // 2
        position = first + lax.broadcasted_iota(jnp.int32, values.shape, 1)
        recorded = (position < begin) | (position >= begin + width - length)
        return jnp.where(recorded, values, 0.0)

    load.wait()
    total = jnp.zeros((rows, PAD), f32)
    for ch in range(CHUNKS):
        piece = gap(raw[:, ch * chunk : (ch + 1) * chunk], t, ch * chunk)
        cross[0, ch] = piece.astype(bf16)
        for i in range(chunk // PAD):
            tile = piece[:, i * PAD : (i + 1) * PAD]
            total = total + tile * tile
    esend[...] = total
    pl.semaphore_wait(barrier, len(peers))

    energy = []
    for i in range(1, nt):
        copy = pltpu.make_async_remote_copy(
            esend, erecv.at[i], esend_sem.at[i], erecv_sem.at[i],
            device_id=at_tm(i), device_id_type=MESH,
        )
        copy.start()
        energy.append(copy)
    to_next = pltpu.make_async_remote_copy(
        raw.at[:, pl.ds(width - PAD, PAD)], edge.at[0], hsend_sem.at[0], hrecv_sem.at[0],
        device_id=at_tm(1), device_id_type=MESH,
    )
    to_previous = pltpu.make_async_remote_copy(
        raw.at[:, pl.ds(0, PAD)], edge.at[1], hsend_sem.at[1], hrecv_sem.at[1],
        device_id=at_tm(nt - 1), device_id_type=MESH,
    )
    to_next.start()
    to_previous.start()
    crossing = []
    for ch in range(CHUNKS):
        copy = pltpu.make_async_remote_copy(
            cross.at[0, ch], cross.at[1, ch], csend_sem.at[ch], crecv_sem.at[ch],
            device_id=flip(half_mask), device_id_type=MESH,
        )
        copy.start()
        crossing.append(copy)

    summed = lengths_ref[0]
    for i in range(1, nt):
        summed = summed + lengths_ref[i]
    count = jnp.full((1, 1), summed, jnp.int32).astype(f32)
    padded[:, :PAD] = jnp.zeros((rows, PAD), bf16)
    padded[:, PAD + width :] = jnp.zeros((rows, PAD), bf16)

    for copy in energy:
        copy.wait_recv()
    for i in range(1, nt):
        total = total + erecv[i]
    power = jnp.sum(total, axis=1, keepdims=True) / count + 1e-06
    root = jnp.sqrt(power)

    def whiten(values):
        return (values / root).astype(bf16)

    norms[0, 0] = jnp.broadcast_to(1.0 / root, (rows, PAD))

    def pass_norm(stage, mask):
        copy = pltpu.make_async_remote_copy(
            norms.at[stage, 0], norms.at[stage, 1], nsend_sem.at[stage], nrecv_sem.at[stage],
            device_id=flip(mask), device_id_type=MESH,
        )
        copy.start()
        return copy

    normed = [pass_norm(0, half_mask)]
    for ch in range(CHUNKS):
        piece = whiten(gap(raw[:, ch * chunk : (ch + 1) * chunk], t, ch * chunk))
        ext[:, PAD + ch * chunk : PAD + (ch + 1) * chunk] = piece.astype(f32)
        padded[:, PAD + ch * chunk : PAD + (ch + 1) * chunk] = piece

    to_next.wait_recv()
    to_previous.wait_recv()
    before = whiten(gap(edge[0], lax.rem(t + nt - 1, nt), width - PAD)).astype(f32)
    after = whiten(gap(edge[1], lax.rem(t + 1, nt), 0)).astype(f32)
    ext[:, :PAD] = jnp.where(t > 0, before, 0.0)
    ext[:, PAD + width :] = jnp.where(t < nt - 1, after, 0.0)

    top = FINE * (COARSE - 1) - HALF
    for pair in range(rows // 2):
        both = []
        for c in (2 * pair, 2 * pair + 1):
            row = jnp.broadcast_to(ext[c : c + 1, :], (FINE, width + 2 * PAD))
            rolled = pltpu.roll(
                row, width + 2 * PAD - (PAD - top), 1, stride=1, stride_axis=0
            )
            both.append(rolled[:, :span])
        lhs[2 * FINE * pair : 2 * FINE * (pair + 1), :] = jnp.concatenate(both, axis=0).astype(bf16)

    sends = []

    def correlate(slot):
        for a in range(COARSE):
            offset = PAD - FINE * (COARSE - 1) + FINE * a
            rhs[a * rows : (a + 1) * rows, :] = padded[:, offset : offset + span]
        product = lax.dot_general(
            lhs[...], rhs[...], (((1,), (1,)), ((), ())), preferred_element_type=f32
        )
        part[slot] = product.astype(bf16).reshape(nt, share * FINE, COARSE * rows)
        for i in range(1, nt):
            copy = pltpu.make_async_remote_copy(
                part.at[slot, lax.rem(t + i, nt)], parts.at[slot, i],
                psend_sem.at[slot, i], precv_sem.at[slot, i],
                device_id=at_tm(i), device_id_type=MESH,
            )
            copy.start()
            sends.append(copy)

    correlate(0)

    first_mask = partners_ref[0, 0]
    second_mask = partners_ref[1, 0]
    swapped = first_mask != half_mask
    other = jnp.where(swapped, first_mask, second_mask)
    crossed = other >= half_mask

    stages = [[] for _ in range(bits)]

    def forward(stage, ch, piece):
        hops[stage, 0, ch] = piece
        copy = pltpu.make_async_remote_copy(
            hops.at[stage, 0, ch], hops.at[stage, 1, ch],
            bsend_sem.at[stage, ch], brecv_sem.at[stage, ch],
            device_id=flip(1 << stage), device_id_type=MESH,
        )
        copy.start()
        stages[stage].append(copy)

    def place(ch, piece):
        padded[:, PAD + ch * chunk : PAD + (ch + 1) * chunk] = piece

    for ch in range(CHUNKS):
        crossing[ch].wait_recv()
        arrived = cross[1, ch]
        forward(0, ch, jnp.where(crossed, arrived, cross[0, ch]))
        place(ch, arrived)
    normed[0].wait_recv()
    norms[1, 0] = jnp.where(crossed, norms[0, 1], norms[0, 0])
    normed.append(pass_norm(1, 1))
    correlate(1)
    for stage in range(bits):
        taken = lax.rem(other // (1 << stage), 2) == 1
        for ch in range(CHUNKS):
            stages[stage][ch].wait_recv()
            piece = jnp.where(taken, hops[stage, 1, ch], hops[stage, 0, ch])
            if stage < bits - 1:
                forward(stage + 1, ch, piece)
            else:
                place(ch, piece)
        normed[stage + 1].wait_recv()
        factor = jnp.where(taken, norms[stage + 1, 1], norms[stage + 1, 0])
        if stage < bits - 1:
            norms[stage + 2, 0] = factor
            normed.append(pass_norm(stage + 2, 2 << stage))
    correlate(2)

    scale = 1.0 / jnp.sqrt(count)
    results = []
    for slot in range(ROUNDS + 1):
        mine = part[slot, t].astype(f32)
        for i in range(1, nt):
            sends[slot * (nt - 1) + i - 1].wait_recv()
            mine = mine + parts[slot, i].astype(f32)
        results.append(mine * scale)
    ordered = [
        results[0],
        jnp.where(swapped, results[2], results[1]),
        jnp.where(swapped, results[1], results[2]),
    ]
    near = norms[0, 1]
    factors = jnp.concatenate(
        [
            jnp.ones((rows, PAD), f32),
            jnp.where(swapped, factor, near),
            jnp.where(swapped, near, factor),
        ],
        axis=0,
    )
    fine = lax.broadcasted_iota(jnp.int32, (FINE, rows), 0)
    column = lax.broadcasted_iota(jnp.int32, (FINE, rows), 1)
    for c in range(share):
        lags = []
        for a in range(COARSE):
            tiles = [
                x[c * FINE : (c + 1) * FINE, a * rows : (a + 1) * rows] for x in ordered
            ]
            if a == HALF // FINE:
                killed = (fine == HALF % FINE) & (column == t * share + c)
                tiles[0] = jnp.where(killed, 0.0, tiles[0])
            spare = PAD - len(tiles) * rows
            lags.append(jnp.concatenate(tiles + [jnp.zeros((FINE, spare), f32)], axis=1))
        lags.append(jnp.zeros((PAD - FINE * COARSE, PAD), f32))
        turned = jnp.concatenate(lags, axis=0).T
        out_ref[c] = (turned[: len(ordered) * rows] * factors)[:, :LAGS]

    for copy in energy + [to_next, to_previous] + crossing + sum(stages, []) + normed + sends:
        copy.wait_send()


def shards(nb, nt, traces, partners, lengths):
    rows, width = traces.shape
    share = rows // nt
    bits = nb.bit_length() - 2
    chunk = width // CHUNKS
    span = width + PAD
    f32, bf16 = jnp.float32, jnp.bfloat16
    dma = pltpu.SemaphoreType.DMA
    slots = ROUNDS + 1
    found = pl.pallas_call(
        functools.partial(kernel, nb, nt, rows, width),
        out_shape=jax.ShapeDtypeStruct((share, slots * rows, LAGS), f32),
        in_specs=[
            pl.BlockSpec(memory_space=pl.ANY),
            pl.BlockSpec(memory_space=pltpu.SMEM),
            pl.BlockSpec(memory_space=pltpu.SMEM),
        ],
        out_specs=pl.BlockSpec(memory_space=pltpu.VMEM),
        scratch_shapes=[
            pltpu.VMEM((rows, width), f32),
            pltpu.VMEM((2, rows, PAD), f32),
            pltpu.VMEM((rows, PAD), f32),
            pltpu.VMEM((nt, rows, PAD), f32),
            pltpu.VMEM((rows, width + 2 * PAD), f32),
            pltpu.VMEM((rows * FINE, span), bf16),
            pltpu.VMEM((COARSE * rows, span), bf16),
            pltpu.VMEM((rows, width + 2 * PAD), bf16),
            pltpu.VMEM((2, CHUNKS, rows, chunk), bf16),
            pltpu.VMEM((bits, 2, CHUNKS, rows, chunk), bf16),
            pltpu.VMEM((bits + 1, 2, rows, PAD), f32),
            pltpu.VMEM((slots, nt, share * FINE, COARSE * rows), bf16),
            pltpu.VMEM((slots, nt, share * FINE, COARSE * rows), bf16),
            dma,
            dma((nt,)), dma((nt,)),
            dma((2,)), dma((2,)),
            dma((CHUNKS,)), dma((CHUNKS,)),
            dma((bits, CHUNKS)), dma((bits, CHUNKS)),
            dma((bits + 1,)), dma((bits + 1,)),
            dma((slots, nt)), dma((slots, nt)),
        ],
        compiler_params=pltpu.CompilerParams(collective_id=0, has_side_effects=True),
    )(traces, partners, lengths)
    found = found.reshape(share, slots, rows, LAGS)
    return jnp.transpose(found, (0, 3, 1, 2))


def solution(mesh):
    placed = (P("block", "tm"), P(), P())
    return jax.shard_map(
        functools.partial(shards, mesh.shape["block"], mesh.shape["tm"]),
        mesh=mesh,
        in_specs=placed,
        out_specs=P(("block", "tm"), None, None, None),
        check_vma=False,
    )
```

profile of v0, /device:TPU:1, one launch (start us, length us, event | category | flops | bytes accessed | tf_op | source)
XLA Modules:
  0.0 26.1 jit_solution(16918342510606358368)
XLA Ops:
  0.0 24.3 %shard_map.37 = f32[8,96,101]{2,1,0:T(8,128)} custom-call(f32[32,2048]{1,0:T(8,128)} %traces_ref.1, s32[2,8]{1,0:T(2,128)} %partners_ref.1, s32[4]{0:T(128)} %lengths_ref.1), custom_call_target="tpu_custom_call" | custom-call | tf_op jit(solution)/shard_map/pallas_call | solution.py:267
  24.3 1.8 %copy.5 = f32[8,101,3,32]{1,3,2,0:T(8,128)} copy(f32[8,101,3,32]{1,3,2,0:T(8,128)} %bitcast.3) | data formatting | bytes 620544
where the time goes:
time: 26.5 us; the launch traced here: 26.1 us
  Pallas kernels  24.3 us (92%)
  local copies, waits for them, and re-layouts  1.77 us (7%)
    pallas_call x1, Pallas kernels, shards(): pl.pallas_call(functools.partial(kernel, nb, nt, rows, width), out_shape=...  24.3 us
    unnamed x1, local copies, waits for them, and re-layouts  1.77 us

commit v1 on v0

--- a/solution.py
+++ b/solution.py
@@ -14,7 +14,13 @@
 COARSE = 13
 PAD = 128
 CHUNKS = 8
+STOPS = (3, 5, 6, 7)
 MESH = pl.DeviceIdType.MESH
+
+
+def routes(nb):
+    bits = nb.bit_length() - 2
+    return [(low, min(4, 2 << (bits - 1 - low))) for low in range(0, bits, 2)]
 
 
 def kernel(
@@ -27,7 +33,6 @@
 ):
     b = lax.axis_index("block")
     t = lax.axis_index("tm")
-    bits = nb.bit_length() - 2
     half_mask = nb // 2
     share = rows // nt
     chunk = width // CHUNKS
@@ -38,14 +43,21 @@
         return (b, lax.rem(t + i, nt))
 
     def flip(mask):
-        size = 2 * mask
-        low = lax.rem(b, size)
-        return (b - low + lax.rem(low + mask, size), t)
+        target = b
+        for i in range(nb.bit_length() - 1):
+            if mask >> i & 1:
+                size = 2 << i
+                low = lax.rem(target, size)
+                target = target - low + lax.rem(low + (1 << i), size)
+        return (target, t)
+
+    digits = routes(nb)
 
     barrier = pltpu.get_barrier_semaphore()
     load = pltpu.make_async_copy(traces_ref, raw, load_sem)
     load.start()
-    peers = [at_tm(i) for i in range(1, nt)] + [flip(1 << i) for i in range(bits + 1)]
+    peers = [at_tm(i) for i in range(1, nt)] + [flip(half_mask)]
+    peers += [flip(m << low) for low, ways in digits for m in range(1, ways)]
     for peer in peers:
         pl.semaphore_signal(barrier, inc=1, device_id=peer, device_id_type=MESH)
 
@@ -113,15 +125,19 @@
 
     norms[0, 0] = jnp.broadcast_to(1.0 / root, (rows, PAD))
 
-    def pass_norm(stage, mask):
-        copy = pltpu.make_async_remote_copy(
-            norms.at[stage, 0], norms.at[stage, 1], nsend_sem.at[stage], nrecv_sem.at[stage],
-            device_id=flip(mask), device_id_type=MESH,
-        )
-        copy.start()
-        return copy
-
-    normed = [pass_norm(0, half_mask)]
+    def pass_norm(stage, masks):
+        copies = []
+        for i, mask in enumerate(masks):
+            copy = pltpu.make_async_remote_copy(
+                norms.at[stage, 0], norms.at[stage, 1 + i],
+                nsend_sem.at[stage, i], nrecv_sem.at[stage, i],
+                device_id=flip(mask), device_id_type=MESH,
+            )
+            copy.start()
+            copies.append(copy)
+        return copies
+
+    normed = [pass_norm(0, [half_mask])]
     for ch in range(CHUNKS):
         piece = whiten(gap(raw[:, ch * chunk : (ch + 1) * chunk], t, ch * chunk))
         ext[:, PAD + ch * chunk : PAD + (ch + 1) * chunk] = piece.astype(f32)
@@ -147,13 +163,16 @@
 
     sends = []
 
-    def correlate(slot):
+    def multiply(first, last):
         for a in range(COARSE):
             offset = PAD - FINE * (COARSE - 1) + FINE * a
-            rhs[a * rows : (a + 1) * rows, :] = padded[:, offset : offset + span]
-        product = lax.dot_general(
-            lhs[...], rhs[...], (((1,), (1,)), ((), ())), preferred_element_type=f32
+            rhs[a * rows : (a + 1) * rows, first:last] = padded[:, offset + first : offset + last]
+        return lax.dot_general(
+            lhs[:, first:last], rhs[:, first:last],
+            (((1,), (1,)), ((), ())), preferred_element_type=f32,
         )
+
+    def scatter(slot, product):
         part[slot] = product.astype(bf16).reshape(nt, share * FINE, COARSE * rows)
         for i in range(1, nt):
             copy = pltpu.make_async_remote_copy(
@@ -164,7 +183,7 @@
             copy.start()
             sends.append(copy)
 
-    correlate(0)
+    scatter(0, multiply(0, span))
 
     first_mask = partners_ref[0, 0]
     second_mask = partners_ref[1, 0]
@@ -172,45 +191,67 @@
     other = jnp.where(swapped, first_mask, second_mask)
     crossed = other >= half_mask
 
-    stages = [[] for _ in range(bits)]
+    hop_copies = []
+    arrivals = {}
 
     def forward(stage, ch, piece):
+        low, ways = digits[stage]
         hops[stage, 0, ch] = piece
-        copy = pltpu.make_async_remote_copy(
-            hops.at[stage, 0, ch], hops.at[stage, 1, ch],
-            bsend_sem.at[stage, ch], brecv_sem.at[stage, ch],
-            device_id=flip(1 << stage), device_id_type=MESH,
-        )
-        copy.start()
-        stages[stage].append(copy)
+        for m in range(ways - 1, 0, -1):
+            copy = pltpu.make_async_remote_copy(
+                hops.at[stage, 0, ch], hops.at[stage, m, ch],
+                bsend_sem.at[stage, m, ch], brecv_sem.at[stage, m, ch],
+                device_id=flip(m << low), device_id_type=MESH,
+            )
+            copy.start()
+            hop_copies.append(copy)
+            arrivals[stage, m, ch] = copy
+
+    def choose(stage, choices):
+        low, ways = digits[stage]
+        digit = lax.rem(other // (1 << low), ways)
+        piece = choices[0]
+        for m in range(1, ways):
+            piece = jnp.where(digit == m, choices[m], piece)
+        return piece
 
     def place(ch, piece):
         padded[:, PAD + ch * chunk : PAD + (ch + 1) * chunk] = piece
+
+    def through(ch):
+        edge = (ch + 1) * chunk
+        return span if ch == CHUNKS - 1 else edge
 
     for ch in range(CHUNKS):
         crossing[ch].wait_recv()
         arrived = cross[1, ch]
         forward(0, ch, jnp.where(crossed, arrived, cross[0, ch]))
         place(ch, arrived)
-    normed[0].wait_recv()
-    norms[1, 0] = jnp.where(crossed, norms[0, 1], norms[0, 0])
-    normed.append(pass_norm(1, 1))
-    correlate(1)
-    for stage in range(bits):
-        taken = lax.rem(other // (1 << stage), 2) == 1
+    scatter(1, multiply(0, span))
+    normed[0][0].wait_recv()
+    factor = jnp.where(crossed, norms[0, 1], norms[0, 0])
+    for stage, (low, ways) in enumerate(digits):
+        norms[stage + 1, 0] = factor
+        normed.append(pass_norm(stage + 1, [m << low for m in range(1, ways)]))
+        total = None
+        done = 0
         for ch in range(CHUNKS):
-            stages[stage][ch].wait_recv()
-            piece = jnp.where(taken, hops[stage, 1, ch], hops[stage, 0, ch])
-            if stage < bits - 1:
+            for m in range(1, ways):
+                arrivals[stage, m, ch].wait_recv()
+            piece = choose(stage, [hops[stage, m, ch] for m in range(ways)])
+            if stage < len(digits) - 1:
                 forward(stage + 1, ch, piece)
-            else:
-                place(ch, piece)
-        normed[stage + 1].wait_recv()
-        factor = jnp.where(taken, norms[stage + 1, 1], norms[stage + 1, 0])
-        if stage < bits - 1:
-            norms[stage + 2, 0] = factor
-            normed.append(pass_norm(stage + 2, 2 << stage))
-    correlate(2)
+                continue
+            place(ch, piece)
+            if ch in STOPS:
+                product = multiply(done, through(ch))
+                total = product if total is None else total + product
+                done = through(ch)
+        if stage == len(digits) - 1:
+            scatter(2, total)
+        for copy in normed[stage + 1]:
+            copy.wait_recv()
+        factor = choose(stage, [norms[stage + 1, m] for m in range(ways)])
 
     scale = 1.0 / jnp.sqrt(count)
     results = []
@@ -251,14 +292,15 @@
         turned = jnp.concatenate(lags, axis=0).T
         out_ref[c] = (turned[: len(ordered) * rows] * factors)[:, :LAGS]
 
-    for copy in energy + [to_next, to_previous] + crossing + sum(stages, []) + normed + sends:
+    for copy in energy + [to_next, to_previous] + crossing + hop_copies + sum(normed, []) + sends:
         copy.wait_send()
 
 
 def shards(nb, nt, traces, partners, lengths):
     rows, width = traces.shape
     share = rows // nt
-    bits = nb.bit_length() - 2
+    digits = routes(nb)
+    depth = len(digits)
     chunk = width // CHUNKS
     span = width + PAD
     f32, bf16 = jnp.float32, jnp.bfloat16
@@ -283,16 +325,16 @@
             pltpu.VMEM((COARSE * rows, span), bf16),
             pltpu.VMEM((rows, width + 2 * PAD), bf16),
             pltpu.VMEM((2, CHUNKS, rows, chunk), bf16),
-            pltpu.VMEM((bits, 2, CHUNKS, rows, chunk), bf16),
-            pltpu.VMEM((bits + 1, 2, rows, PAD), f32),
+            pltpu.VMEM((depth, 4, CHUNKS, rows, chunk), bf16),
+            pltpu.VMEM((depth + 1, 4, rows, PAD), f32),
             pltpu.VMEM((slots, nt, share * FINE, COARSE * rows), bf16),
             pltpu.VMEM((slots, nt, share * FINE, COARSE * rows), bf16),
             dma,
             dma((nt,)), dma((nt,)),
             dma((2,)), dma((2,)),
             dma((CHUNKS,)), dma((CHUNKS,)),
-            dma((bits, CHUNKS)), dma((bits, CHUNKS)),
-            dma((bits + 1,)), dma((bits + 1,)),
+            dma((depth, 4, CHUNKS)), dma((depth, 4, CHUNKS)),
+            dma((depth + 1, 3)), dma((depth + 1, 3)),
             dma((slots, nt)), dma((slots, nt)),
         ],
         compiler_params=pltpu.CompilerParams(collective_id=0, has_side_effects=True),

time: 26.5 us -> 28.8 us (1.087)
  Pallas kernels: 24.3 us -> 26.8 us
    pallas_call x1, Pallas kernels: 24.3 us -> 26.8 us  [shards(): pl.pallas_call(functools.partial(kernel, nb, nt, rows, width), out_shape=...]
where the time goes in v1:
time: 28.8 us; the launch traced here: 28.6 us
  Pallas kernels  26.8 us (93%)
  local copies, waits for them, and re-layouts  1.77 us (6%)
    pallas_call x1, Pallas kernels, shards(): pl.pallas_call(functools.partial(kernel, nb, nt, rows, width), out_shape=...  26.8 us
    unnamed x1, local copies, waits for them, and re-layouts  1.77 us

profile of v1, /device:TPU:1, one launch (start us, length us, event | category | flops | bytes accessed | tf_op | source)
XLA Modules:
  0.0 28.6 jit_solution(10917858895520791202)
XLA Ops:
  0.0 26.8 %shard_map.37 = f32[8,96,101]{2,1,0:T(8,128)} custom-call(f32[32,2048]{1,0:T(8,128)} %traces_ref.1, s32[2,8]{1,0:T(2,128)} %partners_ref.1, s32[4]{0:T(128)} %lengths_ref.1), custom_call_target="tpu_custom_call" | custom-call | tf_op jit(solution)/shard_map/pallas_call | solution.py:309
  26.8 1.8 %copy.5 = f32[8,101,3,32]{1,3,2,0:T(8,128)} copy(f32[8,101,3,32]{1,3,2,0:T(8,128)} %bitcast.3) | data formatting | bytes 620544

commit v2 on v0

--- a/solution.py
+++ b/solution.py
@@ -266,7 +266,7 @@
     slots = ROUNDS + 1
     found = pl.pallas_call(
         functools.partial(kernel, nb, nt, rows, width),
-        out_shape=jax.ShapeDtypeStruct((share, slots * rows, LAGS), f32),
+        out_shape=pltpu.VMEM((share, slots * rows, LAGS), f32),
         in_specs=[
             pl.BlockSpec(memory_space=pl.ANY),
             pl.BlockSpec(memory_space=pltpu.SMEM),

time: 26.5 us -> 24.7 us (0.932)
  local copies, waits for them, and re-layouts: 1.77 us -> 0.75 us
  Pallas kernels: 24.3 us -> 23.6 us
    unnamed x1, local copies, waits for them, and re-layouts: 1.77 us -> 0.75 us
    pallas_call x1, Pallas kernels: 24.3 us -> 23.6 us  [shards(): pl.pallas_call(functools.partial(kernel, nb, nt, rows, width), out_shape=...]
where the time goes in v2:
time: 24.7 us; the launch traced here: 24.3 us
  Pallas kernels  23.6 us (96%)
  local copies, waits for them, and re-layouts  0.75 us (3%)
    pallas_call x1, Pallas kernels, shards(): pl.pallas_call(functools.partial(kernel, nb, nt, rows, width), out_shape=...  23.6 us
    unnamed x1, local copies, waits for them, and re-layouts  0.75 us

profile of v2, /device:TPU:1, one launch (start us, length us, event | category | flops | bytes accessed | tf_op | source)
XLA Modules:
  0.0 24.3 jit_solution(13004177863072593991)
XLA Ops:
  0.0 23.6 %shard_map.37 = f32[8,96,101]{2,1,0:T(8,128)S(1)} custom-call(f32[32,2048]{1,0:T(8,128)} %traces_ref.1, s32[2,8]{1,0:T(2,128)} %partners_ref.1, s32[4]{0:T(128)} %lengths_ref.1), custom_call_target="tpu_custom_call" | custom-call | tf_op jit(solution)/shard_map/pallas_call | solution.py:267
  23.6 0.7 %copy.5 = f32[8,101,3,32]{1,3,2,0:T(8,128)} copy(f32[8,101,3,32]{1,3,2,0:T(8,128)S(1)} %bitcast.3) | data formatting | bytes 620544

commit v3 on v2

--- a/solution.py
+++ b/solution.py
@@ -205,10 +205,9 @@
                 forward(stage + 1, ch, piece)
             else:
                 place(ch, piece)
-        normed[stage + 1].wait_recv()
-        factor = jnp.where(taken, norms[stage + 1, 1], norms[stage + 1, 0])
         if stage < bits - 1:
-            norms[stage + 2, 0] = factor
+            normed[stage + 1].wait_recv()
+            norms[stage + 2, 0] = jnp.where(taken, norms[stage + 1, 1], norms[stage + 1, 0])
             normed.append(pass_norm(stage + 2, 2 << stage))
     correlate(2)
 
@@ -226,6 +225,8 @@
         jnp.where(swapped, results[1], results[2]),
     ]
     near = norms[0, 1]
+    normed[bits].wait_recv()
+    factor = jnp.where(taken, norms[bits, 1], norms[bits, 0])
     factors = jnp.concatenate(
         [
             jnp.ones((rows, PAD), f32),

time: 24.7 us -> 24.5 us (level)
  no operation moved by 1% of the time
where the time goes in v3:
time: 24.5 us; the launch traced here: 24.1 us
  Pallas kernels  23.4 us (96%)
  local copies, waits for them, and re-layouts  0.75 us (3%)
    pallas_call x1, Pallas kernels, shards(): pl.pallas_call(functools.partial(kernel, nb, nt, rows, width), out_shape=...  23.4 us
    unnamed x1, local copies, waits for them, and re-layouts  0.75 us

profile of v3, /device:TPU:1, one launch (start us, length us, event | category | flops | bytes accessed | tf_op | source)
XLA Modules:
  0.0 24.1 jit_solution(13419835891846112934)
XLA Ops:
  0.0 23.4 %shard_map.37 = f32[8,96,101]{2,1,0:T(8,128)S(1)} custom-call(f32[32,2048]{1,0:T(8,128)} %traces_ref.1, s32[2,8]{1,0:T(2,128)} %partners_ref.1, s32[4]{0:T(128)} %lengths_ref.1), custom_call_target="tpu_custom_call" | custom-call | tf_op jit(solution)/shard_map/pallas_call | solution.py:268
  23.4 0.7 %copy.5 = f32[8,101,3,32]{1,3,2,0:T(8,128)} copy(f32[8,101,3,32]{1,3,2,0:T(8,128)S(1)} %bitcast.3) | data formatting | bytes 620544

commit v4 on v3

--- a/solution.py
+++ b/solution.py
@@ -212,45 +212,58 @@
     correlate(2)
 
     scale = 1.0 / jnp.sqrt(count)
-    results = []
-    for slot in range(ROUNDS + 1):
+    full = COARSE * rows // PAD
+    quad = PAD // rows
+    lane = lax.broadcasted_iota(jnp.int32, (full * FINE, PAD), 1)
+
+    def gathered(slot):
         mine = part[slot, t].astype(f32)
         for i in range(1, nt):
             sends[slot * (nt - 1) + i - 1].wait_recv()
             mine = mine + parts[slot, i].astype(f32)
-        results.append(mine * scale)
-    ordered = [
-        results[0],
-        jnp.where(swapped, results[2], results[1]),
-        jnp.where(swapped, results[1], results[2]),
-    ]
-    near = norms[0, 1]
+        mine = mine * scale
+        out = []
+        for c0 in range(0, share, quad):
+            blocks = []
+            rests = []
+            for c in range(c0, min(c0 + quad, share)):
+                own = mine[c * FINE : (c + 1) * FINE]
+                blocks.append(jnp.concatenate(
+                    [own[:, j * PAD : (j + 1) * PAD] for j in range(full)], axis=0
+                ))
+                rests.append(own[:, full * PAD :])
+            real = len(blocks)
+            blocks += [jnp.zeros((full * FINE, PAD), f32)] * (quad - real)
+            step = 1
+            while step < quad:
+                odd = lax.rem(lane // (rows * step), 2) == 1
+                for i in range(quad):
+                    if not i & step:
+                        one, two = blocks[i], blocks[i + step]
+                        blocks[i] = jnp.where(odd, pltpu.roll(two, rows * step, 1), one)
+                        blocks[i + step] = jnp.where(odd, two, pltpu.roll(one, PAD - rows * step, 1))
+                step *= 2
+            lags = [
+                blocks[i][j * FINE : (j + 1) * FINE] for j in range(full) for i in range(quad)
+            ]
+            if real < quad:
+                rests.append(jnp.zeros((FINE, PAD - real * rows), f32))
+            lags.append(jnp.concatenate(rests, axis=1))
+            lags.append(jnp.zeros((PAD - FINE * COARSE, PAD), f32))
+            turned = jnp.concatenate(lags, axis=0).T
+            out.append(turned.reshape(quad, rows, PAD)[:real])
+        return jnp.concatenate(out, axis=0)
+
+    shape = (share, rows, PAD)
+    index, column, lag = (lax.broadcasted_iota(jnp.int32, shape, i) for i in range(3))
+    killed = (lag == HALF) & (column == t * share + index)
+    out_ref[:, :rows, :] = jnp.where(killed, 0.0, gathered(0))[:, :, :LAGS]
+    near = gathered(1) * norms[0, 1][None]
     normed[bits].wait_recv()
     factor = jnp.where(taken, norms[bits, 1], norms[bits, 0])
-    factors = jnp.concatenate(
-        [
-            jnp.ones((rows, PAD), f32),
-            jnp.where(swapped, factor, near),
-            jnp.where(swapped, near, factor),
-        ],
-        axis=0,
-    )
-    fine = lax.broadcasted_iota(jnp.int32, (FINE, rows), 0)
-    column = lax.broadcasted_iota(jnp.int32, (FINE, rows), 1)
-    for c in range(share):
-        lags = []
-        for a in range(COARSE):
-            tiles = [
-                x[c * FINE : (c + 1) * FINE, a * rows : (a + 1) * rows] for x in ordered
-            ]
-            if a == HALF // FINE:
-                killed = (fine == HALF % FINE) & (column == t * share + c)
-                tiles[0] = jnp.where(killed, 0.0, tiles[0])
-            spare = PAD - len(tiles) * rows
-            lags.append(jnp.concatenate(tiles + [jnp.zeros((FINE, spare), f32)], axis=1))
-        lags.append(jnp.zeros((PAD - FINE * COARSE, PAD), f32))
-        turned = jnp.concatenate(lags, axis=0).T
-        out_ref[c] = (turned[: len(ordered) * rows] * factors)[:, :LAGS]
+    far = gathered(2) * factor[None]
+    out_ref[:, rows : 2 * rows, :] = jnp.where(swapped, far, near)[:, :, :LAGS]
+    out_ref[:, 2 * rows :, :] = jnp.where(swapped, near, far)[:, :, :LAGS]
 
     for copy in energy + [to_next, to_previous] + crossing + sum(stages, []) + normed + sends:
         copy.wait_send()

time: 24.5 us -> 24.2 us (0.988)
  Pallas kernels: 23.4 us -> 23.1 us
    pallas_call x1, Pallas kernels: 23.4 us -> 23.1 us  [shards(): pl.pallas_call(functools.partial(kernel, nb, nt, rows, width), out_shape=...]
where the time goes in v4:
time: 24.2 us; the launch traced here: 23.9 us
  Pallas kernels  23.1 us (95%)
  local copies, waits for them, and re-layouts  0.75 us (3%)
    pallas_call x1, Pallas kernels, shards(): pl.pallas_call(functools.partial(kernel, nb, nt, rows, width), out_shape=...  23.1 us
    unnamed x1, local copies, waits for them, and re-layouts  0.75 us

profile of v4, /device:TPU:1, one launch (start us, length us, event | category | flops | bytes accessed | tf_op | source)
XLA Modules:
  0.0 23.9 jit_solution(15903420539376839557)
XLA Ops:
  0.0 23.1 %shard_map.37 = f32[8,96,101]{2,1,0:T(8,128)S(1)} custom-call(f32[32,2048]{1,0:T(8,128)} %traces_ref.1, s32[2,8]{1,0:T(2,128)} %partners_ref.1, s32[4]{0:T(128)} %lengths_ref.1), custom_call_target="tpu_custom_call" | custom-call | tf_op jit(solution)/shard_map/pallas_call | solution.py:281
  23.1 0.7 %copy.5 = f32[8,101,3,32]{1,3,2,0:T(8,128)} copy(f32[8,101,3,32]{1,3,2,0:T(8,128)S(1)} %bitcast.3) | data formatting | bytes 620544

commit v5 on v4

--- a/solution.py
+++ b/solution.py
@@ -19,7 +19,7 @@
 
 def kernel(
     nb, nt, rows, width,
-    traces_ref, partners_ref, lengths_ref, out_ref,
+    traces_ref, partners_hbm, lengths_hbm, out_ref, partners_ref, lengths_ref, table_sem,
     raw, edge, esend, erecv, ext, lhs, rhs, padded, cross, hops, norms, part, parts,
     load_sem, esend_sem, erecv_sem, hsend_sem, hrecv_sem,
     csend_sem, crecv_sem, bsend_sem, brecv_sem,
@@ -45,6 +45,10 @@
     barrier = pltpu.get_barrier_semaphore()
     load = pltpu.make_async_copy(traces_ref, raw, load_sem)
     load.start()
+    lengths_load = pltpu.make_async_copy(lengths_hbm, lengths_ref, table_sem.at[0])
+    partners_load = pltpu.make_async_copy(partners_hbm, partners_ref, table_sem.at[1])
+    lengths_load.start()
+    partners_load.start()
     peers = [at_tm(i) for i in range(1, nt)] + [flip(1 << i) for i in range(bits + 1)]
     for peer in peers:
         pl.semaphore_signal(barrier, inc=1, device_id=peer, device_id_type=MESH)
@@ -56,6 +60,7 @@
         recorded = (position < begin) | (position >= begin + width - length)
         return jnp.where(recorded, values, 0.0)
 
+    lengths_load.wait()
     load.wait()
     total = jnp.zeros((rows, PAD), f32)
     for ch in range(CHUNKS):
@@ -166,6 +171,7 @@
 
     correlate(0)
 
+    partners_load.wait()
     first_mask = partners_ref[0, 0]
     second_mask = partners_ref[1, 0]
     swapped = first_mask != half_mask
@@ -283,11 +289,14 @@
         out_shape=pltpu.VMEM((share, slots * rows, LAGS), f32),
         in_specs=[
             pl.BlockSpec(memory_space=pl.ANY),
-            pl.BlockSpec(memory_space=pltpu.SMEM),
-            pl.BlockSpec(memory_space=pltpu.SMEM),
+            pl.BlockSpec(memory_space=pl.ANY),
+            pl.BlockSpec(memory_space=pl.ANY),
         ],
         out_specs=pl.BlockSpec(memory_space=pltpu.VMEM),
         scratch_shapes=[
+            pltpu.SMEM(partners.shape, jnp.int32),
+            pltpu.SMEM(lengths.shape, jnp.int32),
+            dma((2,)),
             pltpu.VMEM((rows, width), f32),
             pltpu.VMEM((2, rows, PAD), f32),
             pltpu.VMEM((rows, PAD), f32),

time: 24.2 us -> 23.5 us (0.971)
  Pallas kernels: 23.1 us -> 22.4 us
    pallas_call x1, Pallas kernels: 23.1 us -> 22.4 us  [shards(): pl.pallas_call(functools.partial(kernel, nb, nt, rows, width), out_shape=...]
where the time goes in v5:
time: 23.5 us; the launch traced here: 23.1 us
  Pallas kernels  22.4 us (95%)
  local copies, waits for them, and re-layouts  0.75 us (3%)
    pallas_call x1, Pallas kernels, shards(): pl.pallas_call(functools.partial(kernel, nb, nt, rows, width), out_shape=...  22.4 us
    unnamed x1, local copies, waits for them, and re-layouts  0.75 us

profile of v5, /device:TPU:1, one launch (start us, length us, event | category | flops | bytes accessed | tf_op | source)
XLA Modules:
  0.0 23.1 jit_solution(7814761588459620960)
XLA Ops:
  0.0 22.4 %shard_map.37 = f32[8,96,101]{2,1,0:T(8,128)S(1)} custom-call(f32[32,2048]{1,0:T(8,128)} %traces_ref.1, s32[2,8]{1,0:T(2,128)} %partners_hbm.1, s32[4]{0:T(128)} %lengths_hbm.1), custom_call_target="tpu_custom_call" | custom-call | tf_op jit(solution)/shard_map/pallas_call | solution.py:287
  22.4 0.7 %copy.5 = f32[8,101,3,32]{1,3,2,0:T(8,128)} copy(f32[8,101,3,32]{1,3,2,0:T(8,128)S(1)} %bitcast.3) | data formatting | bytes 620544

commit v6 on v5

--- a/solution.py
+++ b/solution.py
@@ -14,6 +14,7 @@
 COARSE = 13
 PAD = 128
 CHUNKS = 8
+STOPS = (3, 5, 7)
 MESH = pl.DeviceIdType.MESH
 
 
@@ -43,16 +44,16 @@
         return (b - low + lax.rem(low + mask, size), t)
 
     barrier = pltpu.get_barrier_semaphore()
+    peers = [flip(1 << i) for i in range(bits, -1, -1)] + [at_tm(i) for i in range(1, nt)]
+    for peer in peers:
+        pl.semaphore_signal(barrier, inc=1, device_id=peer, device_id_type=MESH)
+
     load = pltpu.make_async_copy(traces_ref, raw, load_sem)
     load.start()
     lengths_load = pltpu.make_async_copy(lengths_hbm, lengths_ref, table_sem.at[0])
     partners_load = pltpu.make_async_copy(partners_hbm, partners_ref, table_sem.at[1])
     lengths_load.start()
     partners_load.start()
-    peers = [at_tm(i) for i in range(1, nt)] + [flip(1 << i) for i in range(bits + 1)]
-    for peer in peers:
-        pl.semaphore_signal(barrier, inc=1, device_id=peer, device_id_type=MESH)
-
     def gap(values, index, first):
         length = lengths_ref[index]
         begin = length // 2
@@ -152,13 +153,19 @@
 
     sends = []
 
-    def correlate(slot):
+    def multiply(first, last):
         for a in range(COARSE):
             offset = PAD - FINE * (COARSE - 1) + FINE * a
-            rhs[a * rows : (a + 1) * rows, :] = padded[:, offset : offset + span]
-        product = lax.dot_general(
-            lhs[...], rhs[...], (((1,), (1,)), ((), ())), preferred_element_type=f32
-        )
+            rhs[a * rows : (a + 1) * rows, first:last] = padded[:, offset + first : offset + last]
+        return lax.dot_general(
+            lhs[:, first:last], rhs[:, first:last],
+            (((1,), (1,)), ((), ())), preferred_element_type=f32,
+        )
+
+    def correlate(slot):
+        scatter(slot, multiply(0, span))
+
+    def scatter(slot, product):
         part[slot] = product.astype(bf16).reshape(nt, share * FINE, COARSE * rows)
         for i in range(1, nt):
             copy = pltpu.make_async_remote_copy(
@@ -178,6 +185,8 @@
     other = jnp.where(swapped, first_mask, second_mask)
     crossed = other >= half_mask
 
+    ends = [0]
+    pieces = []
     stages = [[] for _ in range(bits)]
 
     def forward(stage, ch, piece):
@@ -211,11 +220,15 @@
                 forward(stage + 1, ch, piece)
             else:
                 place(ch, piece)
+                if ch in STOPS:
+                    done = ends[-1]
+                    ends.append(span if ch == CHUNKS - 1 else (ch + 1) * chunk)
+                    pieces.append(multiply(done, ends[-1]))
         if stage < bits - 1:
             normed[stage + 1].wait_recv()
             norms[stage + 2, 0] = jnp.where(taken, norms[stage + 1, 1], norms[stage + 1, 0])
             normed.append(pass_norm(stage + 2, 2 << stage))
-    correlate(2)
+    scatter(2, functools.reduce(jnp.add, pieces))
 
     scale = 1.0 / jnp.sqrt(count)
     full = COARSE * rows // PAD

time: 23.5 us -> 23.4 us (level)
  no operation moved by 1% of the time
where the time goes in v6:
time: 23.4 us; the launch traced here: 23 us
  Pallas kernels  22.2 us (95%)
  local copies, waits for them, and re-layouts  0.75 us (3%)
    pallas_call x1, Pallas kernels, shards(): pl.pallas_call(functools.partial(kernel, nb, nt, rows, width), out_shape=...  22.2 us
    unnamed x1, local copies, waits for them, and re-layouts  0.75 us

profile of v6, /device:TPU:1, one launch (start us, length us, event | category | flops | bytes accessed | tf_op | source)
XLA Modules:
  0.0 23.0 jit_solution(12786245072836183615)
XLA Ops:
  0.0 22.2 %shard_map.37 = f32[8,96,101]{2,1,0:T(8,128)S(1)} custom-call(f32[32,2048]{1,0:T(8,128)} %traces_ref.1, s32[2,8]{1,0:T(2,128)} %partners_hbm.1, s32[4]{0:T(128)} %lengths_hbm.1), custom_call_target="tpu_custom_call" | custom-call | tf_op jit(solution)/shard_map/pallas_call | solution.py:300
  22.2 0.7 %copy.5 = f32[8,101,3,32]{1,3,2,0:T(8,128)} copy(f32[8,101,3,32]{1,3,2,0:T(8,128)S(1)} %bitcast.3) | data formatting | bytes 620544

commit v7 on v6

--- a/solution.py
+++ b/solution.py
@@ -14,7 +14,7 @@
 COARSE = 13
 PAD = 128
 CHUNKS = 8
-STOPS = (3, 5, 7)
+STOPS = (1, 3, 5, 7)
 MESH = pl.DeviceIdType.MESH
 
 

time: 23.4 us -> 23.2 us (level)
  no operation moved by 1% of the time
where the time goes in v7:
time: 23.2 us; the launch traced here: 22.9 us
  Pallas kernels  22.1 us (95%)
  local copies, waits for them, and re-layouts  0.75 us (3%)
    pallas_call x1, Pallas kernels, shards(): pl.pallas_call(functools.partial(kernel, nb, nt, rows, width), out_shape=...  22.1 us
    unnamed x1, local copies, waits for them, and re-layouts  0.75 us

profile of v7, /device:TPU:1, one launch (start us, length us, event | category | flops | bytes accessed | tf_op | source)
XLA Modules:
  0.0 22.9 jit_solution(441188378891905469)
XLA Ops:
  0.0 22.1 %shard_map.37 = f32[8,96,101]{2,1,0:T(8,128)S(1)} custom-call(f32[32,2048]{1,0:T(8,128)} %traces_ref.1, s32[2,8]{1,0:T(2,128)} %partners_hbm.1, s32[4]{0:T(128)} %lengths_hbm.1), custom_call_target="tpu_custom_call" | custom-call | tf_op jit(solution)/shard_map/pallas_call | solution.py:300
  22.1 0.7 %copy.5 = f32[8,101,3,32]{1,3,2,0:T(8,128)} copy(f32[8,101,3,32]{1,3,2,0:T(8,128)S(1)} %bitcast.3) | data formatting | bytes 620544

commit v8 on v7

--- a/solution.py
+++ b/solution.py
@@ -63,15 +63,25 @@
 
     lengths_load.wait()
     load.wait()
+    crossing = []
+    for ch in range(CHUNKS):
+        piece = gap(raw[:, ch * chunk : (ch + 1) * chunk], t, ch * chunk)
+        cross[0, ch] = piece.astype(bf16)
+        if ch == 0:
+            pl.semaphore_wait(barrier, len(peers))
+        copy = pltpu.make_async_remote_copy(
+            cross.at[0, ch], cross.at[1, ch], csend_sem.at[ch], crecv_sem.at[ch],
+            device_id=flip(half_mask), device_id_type=MESH,
+        )
+        copy.start()
+        crossing.append(copy)
     total = jnp.zeros((rows, PAD), f32)
     for ch in range(CHUNKS):
         piece = gap(raw[:, ch * chunk : (ch + 1) * chunk], t, ch * chunk)
-        cross[0, ch] = piece.astype(bf16)
         for i in range(chunk // PAD):
             tile = piece[:, i * PAD : (i + 1) * PAD]
             total = total + tile * tile
     esend[...] = total
-    pl.semaphore_wait(barrier, len(peers))
 
     energy = []
     for i in range(1, nt):
@@ -91,15 +101,6 @@
     )
     to_next.start()
     to_previous.start()
-    crossing = []
-    for ch in range(CHUNKS):
-        copy = pltpu.make_async_remote_copy(
-            cross.at[0, ch], cross.at[1, ch], csend_sem.at[ch], crecv_sem.at[ch],
-            device_id=flip(half_mask), device_id_type=MESH,
-        )
-        copy.start()
-        crossing.append(copy)
-
     summed = lengths_ref[0]
     for i in range(1, nt):
         summed = summed + lengths_ref[i]

time: 23.2 us -> 23.2 us (level)
  no operation moved by 1% of the time
where the time goes in v8:
time: 23.2 us; the launch traced here: 23 us
  Pallas kernels  22.3 us (96%)
  local copies, waits for them, and re-layouts  0.75 us (3%)
    pallas_call x1, Pallas kernels, shards(): pl.pallas_call(functools.partial(kernel, nb, nt, rows, width), out_shape=...  22.3 us
    unnamed x1, local copies, waits for them, and re-layouts  0.75 us

profile of v8, /device:TPU:1, one launch (start us, length us, event | category | flops | bytes accessed | tf_op | source)
XLA Modules:
  0.0 23.0 jit_solution(4214264697947436676)
XLA Ops:
  0.0 22.3 %shard_map.37 = f32[8,96,101]{2,1,0:T(8,128)S(1)} custom-call(f32[32,2048]{1,0:T(8,128)} %traces_ref.1, s32[2,8]{1,0:T(2,128)} %partners_hbm.1, s32[4]{0:T(128)} %lengths_hbm.1), custom_call_target="tpu_custom_call" | custom-call | tf_op jit(solution)/shard_map/pallas_call | solution.py:301
  22.3 0.7 %copy.5 = f32[8,101,3,32]{1,3,2,0:T(8,128)} copy(f32[8,101,3,32]{1,3,2,0:T(8,128)S(1)} %bitcast.3) | data formatting | bytes 620544

commit v9 on v7

--- a/solution.py
+++ b/solution.py
@@ -240,7 +240,6 @@
         for i in range(1, nt):
             sends[slot * (nt - 1) + i - 1].wait_recv()
             mine = mine + parts[slot, i].astype(f32)
-        mine = mine * scale
         out = []
         for c0 in range(0, share, quad):
             blocks = []
@@ -276,11 +275,11 @@
     shape = (share, rows, PAD)
     index, column, lag = (lax.broadcasted_iota(jnp.int32, shape, i) for i in range(3))
     killed = (lag == HALF) & (column == t * share + index)
-    out_ref[:, :rows, :] = jnp.where(killed, 0.0, gathered(0))[:, :, :LAGS]
-    near = gathered(1) * norms[0, 1][None]
+    out_ref[:, :rows, :] = jnp.where(killed, 0.0, gathered(0) * scale)[:, :, :LAGS]
+    near = gathered(1) * (norms[0, 1] * scale)[None]
     normed[bits].wait_recv()
     factor = jnp.where(taken, norms[bits, 1], norms[bits, 0])
-    far = gathered(2) * factor[None]
+    far = gathered(2) * (factor * scale)[None]
     out_ref[:, rows : 2 * rows, :] = jnp.where(swapped, far, near)[:, :, :LAGS]
     out_ref[:, 2 * rows :, :] = jnp.where(swapped, near, far)[:, :, :LAGS]
 

time: 23.2 us -> 23.2 us (level)
  no operation moved by 1% of the time
where the time goes in v9:
time: 23.2 us; the launch traced here: 22.9 us
  Pallas kernels  22.1 us (95%)
  local copies, waits for them, and re-layouts  0.75 us (3%)
    pallas_call x1, Pallas kernels, shards(): pl.pallas_call(functools.partial(kernel, nb, nt, rows, width), out_shape=...  22.1 us
    unnamed x1, local copies, waits for them, and re-layouts  0.75 us

profile of v9, /device:TPU:1, one launch (start us, length us, event | category | flops | bytes accessed | tf_op | source)
XLA Modules:
  0.0 22.9 jit_solution(17035440785746409763)
XLA Ops:
  0.0 22.1 %shard_map.37 = f32[8,96,101]{2,1,0:T(8,128)S(1)} custom-call(f32[32,2048]{1,0:T(8,128)} %traces_ref.1, s32[2,8]{1,0:T(2,128)} %partners_hbm.1, s32[4]{0:T(128)} %lengths_hbm.1), custom_call_target="tpu_custom_call" | custom-call | tf_op jit(solution)/shard_map/pallas_call | solution.py:299
  22.1 0.7 %copy.5 = f32[8,101,3,32]{1,3,2,0:T(8,128)} copy(f32[8,101,3,32]{1,3,2,0:T(8,128)S(1)} %bitcast.3) | data formatting | bytes 620544
